TPU v7x, 512 devices: a whole 4x4x16 slice. The times are simulated.
512 devices in a mesh: gx: 16 (over z), gy: 32 (over y, x, core).
Axes of the slice: x: 4, y: 4, z: 16, core: 2. Of those that a mesh axis runs over, the one named last changes fastest.
Arguments:
- adjoint_guess: float32 [64, 512, 256], P('gx', 'gy'), may hold values from -80 to 80, as said below
- velocity: float32 [3, 64, 16384], P(None, 'gx', 'gy'), may hold values from -1 to 1
- leaf_rate: float32 [64, 16384], P('gx', 'gy'), may hold values from 0.2 to 5
- canopy: int32 [64, 16384], P('gx', 'gy'), may hold values from 0 to 1, as said below
- solid: int32 [64, 16384], P('gx', 'gy'), may hold values from 0 to 1, as said below
- receptors: int32 [8], replicated, may hold values from 0 to 32767
Outputs:
- adjoint_field: float32 [64, 512, 256], P('gx', 'gy')
- residual: float32 [64, 512, 256], P('gx', 'gy')
Inputs may be any that keep to these rules, and one draw needn't show every extreme that they name: `adjoint_guess`: finite values. 1 marks building cells; every horizontal column is solid from the ground up to its building's height. `canopy`: 1 marks tree-crown cells; none is solid.
All inputs are finite; a program needn't handle non-finite values.
Results may differ from a plain program's by a relative error of at most 0.0003.
Values sent between devices are 32-bit elements; how exact they have to be, the bound alone decides.
A program may use at most 64 MiB of HBM per device.

v0:
```python
import jax
import jax.numpy as jnp
from jax import lax
from jax.sharding import PartitionSpec as P

NZ = 32
R = 8
CYCLES = 3
horiz_diff = 4.0
vert_diff = 2.0
decay_rate = 3.5
penalty = 40.0
leaf_gain = 4.0
source_gain = 32.0


def padded_2(shard, sides, width):
    for axis, dim in sides:
        size, length = (lax.axis_size(axis), shard.shape[dim])
        up = [(i, (i + 1) % size) for i in range(size - 1)]
        down = [(j, i) for i, j in up]
        last = lax.slice_in_dim(shard, length - width, length, axis=dim)
        initial = lax.slice_in_dim(shard, 0, width, axis=dim)
        before = lax.ppermute(last, axis, up)
        after = lax.ppermute(initial, axis, down)
        shard = jnp.concatenate([before, shard, after], axis=dim)
    return shard


def coefficient_fields(flows, reaction):
    east_flow = flows[0]
    north_flow = flows[1]
    rise_flow = flows[2]
    couplings = [
        horiz_diff + jax.nn.relu(east_flow),
        horiz_diff + jax.nn.relu(-east_flow),
        horiz_diff + jax.nn.relu(north_flow),
        horiz_diff + jax.nn.relu(-north_flow),
        vert_diff + jax.nn.relu(rise_flow),
        vert_diff + jax.nn.relu(-rise_flow),
    ]
    diagonal = (
        decay_rate
        + reaction
        + couplings[0]
        + couplings[1]
        + couplings[2]
        + couplings[3]
        + couplings[4]
        + couplings[5]
    )
    return [jnp.repeat(piece, R, axis=-1) for piece in [diagonal] + couplings]


def apply_operator(padded, coefficients):
    centre = padded[1:-1, 1:-1]
    zero_lane = jnp.zeros(centre.shape[:-1] + (R,), jnp.float32)
    upper_cells = jnp.concatenate([centre[..., R:], zero_lane], axis=-1)
    lower_cells = jnp.concatenate([zero_lane, centre[..., :-R]], axis=-1)
    diagonal, east_c, west_c, north_c, south_c, upper_c, lower_c = coefficients
    return (
        diagonal * centre
        - east_c * padded[2:, 1:-1]
        - west_c * padded[:-2, 1:-1]
        - north_c * padded[1:-1, 2:]
        - south_c * padded[1:-1, :-2]
        - upper_c * upper_cells
        - lower_c * lower_cells
    )


def per_receptor(first, second):
    return jnp.sum((first * second).reshape(-1, R), axis=0)


def spread_lanes(values):
    return jnp.tile(values, NZ)


def residual_of(image_in, source_in):
    return source_in - image_in


def body(adjoint_guess, velocity, leaf_rate, canopy, solid, receptors):
    rows_dev = adjoint_guess.shape[0]
    cols_dev = adjoint_guess.shape[1]
    total_cols = cols_dev * lax.axis_size("gy")
    row_start = lax.axis_index("gx") * rows_dev
    col_start = lax.axis_index("gy") * cols_dev
    flows = velocity.reshape(3, rows_dev, cols_dev, NZ)
    reaction = (
        penalty * solid.astype(jnp.float32) + leaf_gain * leaf_rate * canopy.astype(jnp.float32)
    ).reshape(rows_dev, cols_dev, NZ)
    coefficients = coefficient_fields(flows, reaction)
    rec_rows = receptors // total_cols
    rec_cols = receptors % total_cols

    def operate(values):
        padded = padded_2(values, (("gx", 0), ("gy", 1)), 1)
        return apply_operator(padded, coefficients)

    global_rows = row_start + jnp.arange(rows_dev, dtype=jnp.int32)
    global_cols = col_start + jnp.arange(cols_dev, dtype=jnp.int32)
    hit_rows = (global_rows[:, None] == rec_rows[None, :]).astype(jnp.float32)
    hit_cols = (global_cols[:, None] == rec_cols[None, :]).astype(jnp.float32)
    receptor_plane = source_gain * hit_rows[:, None, :] * hit_cols[None, :, :]
    ground_lane = jnp.zeros((rows_dev, cols_dev, R), jnp.float32)
    upper_lanes = jnp.zeros((rows_dev, cols_dev, (NZ - 2) * R), jnp.float32)
    source = jnp.concatenate([ground_lane, receptor_plane, upper_lanes], axis=-1)
    iterate = adjoint_guess
    first_image = operate(iterate)
    middle = residual_of(first_image, source)
    second_image = operate(middle)
    residual = middle
    image_dir = second_image
    for cycle_index in range(CYCLES):
        if cycle_index > 0:
            image_dir = operate(residual)
        squares, against = lax.psum(
            (per_receptor(residual, residual), per_receptor(residual, image_dir)), ("gx", "gy")
        )
        alpha_step = squares / against
        halfway = residual - spread_lanes(alpha_step) * image_dir
        turned = operate(halfway)
        along_turn, turn_power = lax.psum(
            (per_receptor(turned, halfway), per_receptor(turned, turned)), ("gx", "gy")
        )
        omega_step = along_turn / turn_power
        iterate = iterate + spread_lanes(alpha_step) * residual + spread_lanes(omega_step) * halfway
        residual = halfway - spread_lanes(omega_step) * turned
    return (iterate, residual)


def solution(mesh):
    return jax.shard_map(
        body,
        mesh=mesh,
        in_specs=(
            P("gx", "gy", None),
            P(None, "gx", "gy"),
            P("gx", "gy"),
            P("gx", "gy"),
            P("gx", "gy"),
            P(),
        ),
        out_specs=(P("gx", "gy", None), P("gx", "gy", None)),
        check_vma=False,
    )
```

profile of v0, /device:TPU:1, one launch (start us, length us, event | category | flops | bytes accessed | tf_op | source)
XLA Modules:
  0.0 755.6 jit_solution(6809923909416197719)
XLA Ops:
  0.6 1.4 fusion.100
  2.0 1.3 collective-permute-start
  3.3 5.6 collective-permute-start.1
  8.9 0.7 fusion.101
  13.5 0.8 broadcast_bitcast_fusion.5
  15.8 0.7 constant_dynamic-update-slice_fusion.2
  17.2 8.3 %collective-permute-start.2 = (f32[6,1,256]{2,1,0:T(1,128)}, f32[6,1,256]{2,1,0:T(1,128)}, u32[]{:S(2)}, u32[]{:S(2)}) collective-permute-start(f32[6,1,256]{2,1,0:T(1,128)} %get-tuple-element.50), channel_id=1, source_target_pairs={{1,0},{2,1},{3,2},{4,3},{5,4},{6,5},{7,6},{8,7},{9,8},{10,9},{11,1... | collective-permute-start | bytes 18440 | tf_op jit(solution)/shard_map/ppermute | solution.py:25
  25.5 1.9 collective-permute-start.3
  31.3 0.8 fusion.85
  32.1 1.3 collective-permute-start.5
  33.4 1.3 collective-permute-start.4
  34.7 3.2 collective-permute-done.4
  37.9 4.2 collective-permute-start.6
  42.1 1.9 collective-permute-start.7
  46.1 111.9 %all-reduce.19 = (f32[8]{0:T(128)S(1)}, f32[8]{0:T(128)S(1)}) all-reduce(f32[8]{0:T(128)S(1)} %reduce_sum.108, f32[8]{0:T(128)S(1)} %reduce_sum.109), channel_id=1, replica_groups=mesh['gx'=16,'gy'=32] {'gx','gy'}, use_global_device_ids=true, to_apply=%region_1.2 | all-reduce | flops 16 | bytes 128 | tf_op jit(solution)/shard_map/psum | solution.py:119
  158.2 1.3 collective-permute-start.9
  159.5 1.3 collective-permute-start.8
  160.8 3.2 collective-permute-done.8
  164.0 4.1 collective-permute-start.10
  168.2 1.9 collective-permute-start.11
  170.2 1.0 collective-permute-done.11
  173.1 104.2 %all-reduce.18 = (f32[8]{0:T(128)S(1)}, f32[8]{0:T(128)S(1)}) all-reduce(f32[8]{0:T(128)S(1)} %reduce_sum.110, f32[8]{0:T(128)S(1)} %reduce_sum.111), channel_id=1, replica_groups=mesh['gx'=16,'gy'=32] {'gx','gy'}, use_global_device_ids=true, to_apply=%region_5.6 | all-reduce | flops 16 | bytes 128 | tf_op jit(solution)/shard_map/psum | solution.py:125
  277.4 1.3 collective-permute-start.13
  278.7 1.3 collective-permute-start.12
  280.0 3.2 collective-permute-done.12
  283.2 3.7 collective-permute-start.14
  286.9 1.9 collective-permute-start.15
  290.9 105.5 %all-reduce.17 = (f32[8]{0:T(128)S(1)}, f32[8]{0:T(128)S(1)}) all-reduce(f32[8]{0:T(128)S(1)} %reduce_sum.112, f32[8]{0:T(128)S(1)} %reduce_sum.113), channel_id=1, replica_groups=mesh['gx'=16,'gy'=32] {'gx','gy'}, use_global_device_ids=true, to_apply=%region_9.10 | all-reduce | flops 16 | bytes 128 | tf_op jit(solution)/shard_map/psum | solution.py:119
  396.5 1.3 collective-permute-start.17
  397.8 1.3 collective-permute-start.16
  399.1 3.2 collective-permute-done.16
  402.3 4.0 collective-permute-start.18
  406.4 1.9 collective-permute-start.19
  408.4 1.0 collective-permute-done.19
  411.3 104.9 %all-reduce.16 = (f32[8]{0:T(128)S(1)}, f32[8]{0:T(128)S(1)}) all-reduce(f32[8]{0:T(128)S(1)} %reduce_sum.114, f32[8]{0:T(128)S(1)} %reduce_sum.115), channel_id=1, replica_groups=mesh['gx'=16,'gy'=32] {'gx','gy'}, use_global_device_ids=true, to_apply=%region_13.14 | all-reduce | flops 16 | bytes 128 | tf_op jit(solution)/shard_map/psum | solution.py:125
  516.3 1.3 collective-permute-start.21
  517.6 1.3 collective-permute-start.20
  518.9 3.2 collective-permute-done.20
  522.1 4.0 collective-permute-start.22
  526.1 2.1 collective-permute-start.23
  530.2 104.8 %all-reduce.15 = (f32[8]{0:T(128)S(1)}, f32[8]{0:T(128)S(1)}) all-reduce(f32[8]{0:T(128)S(1)} %reduce_sum.116, f32[8]{0:T(128)S(1)} %reduce_sum.117), channel_id=1, replica_groups=mesh['gx'=16,'gy'=32] {'gx','gy'}, use_global_device_ids=true, to_apply=%region_17.18 | all-reduce | flops 16 | bytes 128 | tf_op jit(solution)/shard_map/psum | solution.py:119
  635.2 1.3 collective-permute-start.25
  636.4 1.3 collective-permute-start.24
  637.8 3.2 collective-permute-done.24
  640.9 4.0 collective-permute-start.26
  645.0 1.9 collective-permute-start.27
  647.0 1.0 collective-permute-done.27
  649.9 104.9 %all-reduce.14 = (f32[8]{0:T(128)S(1)}, f32[8]{0:T(128)S(1)}) all-reduce(f32[8]{0:T(128)S(1)} %reduce_sum.118, f32[8]{0:T(128)S(1)} %reduce_sum.119), channel_id=1, replica_groups=mesh['gx'=16,'gy'=32] {'gx','gy'}, use_global_device_ids=true, to_apply=%region_21.22 | all-reduce | flops 16 | bytes 128 | tf_op jit(solution)/shard_map/psum | solution.py:125
  (167 shorter events, 23.0 us)
Async XLA Ops:
  0.6 8.3 %copy-start.1 = (f32[4,16,256]{2,1,0:T(8,128)S(1)}, f32[4,16,256]{2,1,0:T(8,128)}, u32[]{:S(2)}) copy-start(f32[4,16,256]{2,1,0:T(8,128)} %param.6) | copy-start | bytes 196612
  2.0 14.5 %collective-permute-start = (f32[1,16,256]{2,1,0:T(8,128)}, f32[1,16,256]{2,1,0:T(8,128)S(1)}, u32[]{:S(2)}, u32[]{:S(2)}) collective-permute-start(f32[1,16,256]{2,1,0:T(8,128)} %get-tuple-element.78), channel_id=1, source_target_pairs={{32,0},{64,32},{96,64},{128,96},{160,128},{192,160},{224,192},{256... | collective-permute-start | bytes 49160 | tf_op jit(solution)/shard_map/ppermute | solution.py:25
  3.3 12.5 %collective-permute-start.1 = (f32[1,16,256]{2,1,0:T(8,128)}, f32[1,16,256]{2,1,0:T(8,128)}, u32[]{:S(2)}, u32[]{:S(2)}) collective-permute-start(f32[1,16,256]{2,1,0:T(8,128)} %get-tuple-element.79), channel_id=1, source_target_pairs={{0,32},{32,64},{64,96},{96,128},{128,160},{160,192},{192,224},{224... | collective-permute-start | bytes 49160 | tf_op jit(solution)/shard_map/ppermute | solution.py:24
  8.9 2.5 copy-start.7
  9.6 1.2 copy-start.14
  9.6 1.7 copy-start.6
  9.6 1.7 copy-start.5
  11.4 0.7 copy-start.4
  14.4 0.7 copy-start.10
  14.4 0.7 copy-start.11
  15.1 0.7 copy-start.12
  15.1 0.7 copy-start.13
  17.2 13.4 %collective-permute-start.2 = (f32[6,1,256]{2,1,0:T(1,128)}, f32[6,1,256]{2,1,0:T(1,128)}, u32[]{:S(2)}, u32[]{:S(2)}) collective-permute-start(f32[6,1,256]{2,1,0:T(1,128)} %get-tuple-element.50), channel_id=1, source_target_pairs={{1,0},{2,1},{3,2},{4,3},{5,4},{6,5},{7,6},{8,7},{9,8},{10,9},{11,1... | collective-permute-start | bytes 18440 | tf_op jit(solution)/shard_map/ppermute | solution.py:25
  25.5 5.1 collective-permute-start.3
  29.4 1.1 copy-start
  30.4 0.8 copy-start.2
  30.4 0.9 copy-start.3
  30.4 0.9 copy-start.9
  30.6 0.7 copy-start.8
  32.1 2.6 collective-permute-start.5
  33.4 4.5 collective-permute-start.4
  37.9 7.1 collective-permute-start.6
  42.1 3.1 collective-permute-start.7
  158.2 2.6 collective-permute-start.9
  159.5 4.5 collective-permute-start.8
  164.0 6.2 collective-permute-start.10
  168.2 3.1 collective-permute-start.11
  277.4 2.6 collective-permute-start.13
  278.7 4.5 collective-permute-start.12
  283.2 6.6 collective-permute-start.14
  286.9 3.1 collective-permute-start.15
  396.5 2.6 collective-permute-start.17
  397.8 4.5 collective-permute-start.16
  402.3 6.0 collective-permute-start.18
  406.4 3.1 collective-permute-start.19
  516.3 2.6 collective-permute-start.21
  517.6 4.5 collective-permute-start.20
  522.1 7.1 collective-permute-start.22
  526.1 3.1 collective-permute-start.23
  635.2 2.6 collective-permute-start.25
  636.4 4.5 collective-permute-start.24
  640.9 6.0 collective-permute-start.26
  645.0 3.1 collective-permute-start.27
where the time goes:
time: 758 us; the launch traced here: 756 us
  blocking collectives  636 us (84%)
  starting transfers between devices  68.4 us (9%)
  waiting for transfers between devices  22.6 us (3%)
  local copies, waits for them, and re-layouts  19.5 us (3%)
  other arithmetic  7.63 us (1%)
    psum x3, blocking collectives, body(): lax.psum((per_receptor(residual, residual), per_receptor(residual, image_...  322 us
    psum x3, blocking collectives, body(): lax.psum((per_receptor(turned, halfway), per_receptor(turned, turned)), (...  314 us
    ppermute x14, starting transfers between devices, padded_2(): after = lax.ppermute(initial, axis, down)  41.4 us
    ppermute x14, starting transfers between devices, padded_2(): before = lax.ppermute(last, axis, up)  27 us
    ppermute x14, waiting for transfers between devices, padded_2(): after = lax.ppermute(initial, axis, down)  19.1 us
  transfers between devices with their start and end apart: 28, of which 11 were waited for; matrix products, arithmetic and copies ran while one was open for 1% of the time, Pallas kernels for 0%

commit v1 on v0

--- a/solution.py
+++ b/solution.py
@@ -123,7 +123,7 @@
         halfway = residual - spread_lanes(alpha_step) * image_dir
         turned = operate(halfway)
         along_turn, turn_power = lax.psum(
-            (per_receptor(turned, halfway), per_receptor(turned, turned)), ("gx", "gy")
+            lax.psum((per_receptor(turned, halfway), per_receptor(turned, turned)), "gx"), "gy"
         )
         omega_step = along_turn / turn_power
         iterate = iterate + spread_lanes(alpha_step) * residual + spread_lanes(omega_step) * halfway

time: 758 us -> 720 us (0.950)
  blocking collectives: 636 us -> 599 us
    psum x3 -> x6, blocking collectives: 314 us -> 279 us  [the longest x3 208 us: body(): lax.psum(lax.psum((per_receptor(turned, halfway), per_receptor(turned, tu...]
  transfers between devices with their start and end apart: 28 -> 28, of which waited for: 11 -> 12; matrix products, arithmetic and copies ran while one was open for 1% -> 2% of each run, Pallas kernels for 0% -> 0%
where the time goes in v1:
time: 720 us; the launch traced here: 718 us
  blocking collectives  599 us (83%)
  starting transfers between devices  67.7 us (9%)
  waiting for transfers between devices  22.7 us (3%)
  local copies, waits for them, and re-layouts  19.5 us (3%)
  other arithmetic  7.57 us (1%)
    psum x3, blocking collectives, body(): lax.psum((per_receptor(residual, residual), per_receptor(residual, image_...  320 us
    psum x3, blocking collectives, body(): lax.psum(lax.psum((per_receptor(turned, halfway), per_receptor(turned, tu...  208 us
    psum x3, blocking collectives, body(): lax.psum((per_receptor(turned, halfway), per_receptor(turned, turned)), '...  70.8 us
    ppermute x14, starting transfers between devices, padded_2(): after = lax.ppermute(initial, axis, down)  40.9 us
    ppermute x14, starting transfers between devices, padded_2(): before = lax.ppermute(last, axis, up)  26.8 us
    ppermute x14, waiting for transfers between devices, padded_2(): after = lax.ppermute(initial, axis, down)  19.1 us
  transfers between devices with their start and end apart: 28, of which 12 were waited for; matrix products, arithmetic and copies ran while one was open for 2% of the time, Pallas kernels for 0%

profile of v1, /device:TPU:1, one launch (start us, length us, event | category | flops | bytes accessed | tf_op | source)
XLA Modules:
  0.0 717.8 jit_solution(13875462248347872372)
XLA Ops:
  0.6 1.4 fusion.100
  2.0 1.3 collective-permute-start
  3.3 5.6 collective-permute-start.1
  13.4 0.8 broadcast_bitcast_fusion.5
  17.1 8.3 %collective-permute-start.2 = (f32[6,1,256]{2,1,0:T(1,128)}, f32[6,1,256]{2,1,0:T(1,128)}, u32[]{:S(2)}, u32[]{:S(2)}) collective-permute-start(f32[6,1,256]{2,1,0:T(1,128)} %get-tuple-element.56), channel_id=1, source_target_pairs={{1,0},{2,1},{3,2},{4,3},{5,4},{6,5},{7,6},{8,7},{9,8},{10,9},{11,1... | collective-permute-start | bytes 18440 | tf_op jit(solution)/shard_map/ppermute | solution.py:25
  25.4 1.9 collective-permute-start.3
  32.1 1.3 collective-permute-start.5
  33.4 1.3 collective-permute-start.4
  34.7 3.2 collective-permute-done.4
  37.8 4.2 collective-permute-start.6
  42.0 1.9 collective-permute-start.7
  46.1 111.9 %all-reduce.16 = (f32[8]{0:T(128)S(1)}, f32[8]{0:T(128)S(1)}) all-reduce(f32[8]{0:T(128)S(1)} %reduce_sum.108, f32[8]{0:T(128)S(1)} %reduce_sum.109), channel_id=1, replica_groups=mesh['gx'=16,'gy'=32] {'gx','gy'}, use_global_device_ids=true, to_apply=%region_1.2 | all-reduce | flops 16 | bytes 128 | tf_op jit(solution)/shard_map/psum | solution.py:119
  158.1 1.3 collective-permute-start.9
  159.4 1.3 collective-permute-start.8
  160.7 3.2 collective-permute-done.8
  163.9 4.1 collective-permute-start.10
  168.1 1.9 collective-permute-start.11
  170.1 1.0 collective-permute-done.11
  173.0 23.5 %all-reduce.22 = (f32[8]{0:T(128)S(1)}, f32[8]{0:T(128)S(1)}) all-reduce(f32[8]{0:T(128)S(1)} %reduce_sum.110, f32[8]{0:T(128)S(1)} %reduce_sum.111), channel_id=1, replica_groups=mesh['gx'=16,'gy'=32] {'gx'}, use_global_device_ids=true, to_apply=%region_5.6 | all-reduce | flops 16 | bytes 128 | tf_op jit(solution)/shard_map/psum | solution.py:126
  196.5 69.4 %all-reduce.19 = (f32[8]{0:T(128)S(1)}, f32[8]{0:T(128)S(1)}) all-reduce(f32[8]{0:T(128)S(1)} %get-tuple-element.24, f32[8]{0:T(128)S(1)} %get-tuple-element.25), channel_id=1, replica_groups=mesh['gx'=16,'gy'=32] {'gy'}, use_global_device_ids=true, to_apply=%region_6.7 | all-reduce | flops 16 | bytes 128 | tf_op jit(solution)/shard_map/psum | solution.py:125
  266.1 1.3 collective-permute-start.13
  267.4 1.3 collective-permute-start.12
  268.7 3.2 collective-permute-done.12
  271.9 3.7 collective-permute-start.14
  275.6 1.9 collective-permute-start.15
  279.6 103.9 %all-reduce.15 = (f32[8]{0:T(128)S(1)}, f32[8]{0:T(128)S(1)}) all-reduce(f32[8]{0:T(128)S(1)} %reduce_sum.112, f32[8]{0:T(128)S(1)} %reduce_sum.113), channel_id=1, replica_groups=mesh['gx'=16,'gy'=32] {'gx','gy'}, use_global_device_ids=true, to_apply=%region_11.12 | all-reduce | flops 16 | bytes 128 | tf_op jit(solution)/shard_map/psum | solution.py:119
  383.7 1.3 collective-permute-start.17
  385.0 1.3 collective-permute-start.16
  386.3 3.2 collective-permute-done.16
  389.5 3.9 collective-permute-start.18
  393.4 1.9 collective-permute-start.19
  395.4 1.0 collective-permute-done.19
  398.3 23.6 %all-reduce.21 = (f32[8]{0:T(128)S(1)}, f32[8]{0:T(128)S(1)}) all-reduce(f32[8]{0:T(128)S(1)} %reduce_sum.114, f32[8]{0:T(128)S(1)} %reduce_sum.115), channel_id=1, replica_groups=mesh['gx'=16,'gy'=32] {'gx'}, use_global_device_ids=true, to_apply=%region_15.16 | all-reduce | flops 16 | bytes 128 | tf_op jit(solution)/shard_map/psum | solution.py:126
  422.0 69.4 %all-reduce.18 = (f32[8]{0:T(128)S(1)}, f32[8]{0:T(128)S(1)}) all-reduce(f32[8]{0:T(128)S(1)} %get-tuple-element.22, f32[8]{0:T(128)S(1)} %get-tuple-element.23), channel_id=1, replica_groups=mesh['gx'=16,'gy'=32] {'gy'}, use_global_device_ids=true, to_apply=%region_16.17 | all-reduce | flops 16 | bytes 128 | tf_op jit(solution)/shard_map/psum | solution.py:125
  491.5 1.3 collective-permute-start.21
  492.8 1.3 collective-permute-start.20
  494.1 3.2 collective-permute-done.20
  497.3 3.7 collective-permute-start.22
  501.0 1.9 collective-permute-start.23
  505.1 104.1 %all-reduce.14 = (f32[8]{0:T(128)S(1)}, f32[8]{0:T(128)S(1)}) all-reduce(f32[8]{0:T(128)S(1)} %reduce_sum.116, f32[8]{0:T(128)S(1)} %reduce_sum.117), channel_id=1, replica_groups=mesh['gx'=16,'gy'=32] {'gx','gy'}, use_global_device_ids=true, to_apply=%region_21.22 | all-reduce | flops 16 | bytes 128 | tf_op jit(solution)/shard_map/psum | solution.py:119
  609.3 1.3 collective-permute-start.25
  610.6 1.3 collective-permute-start.24
  611.9 3.2 collective-permute-done.24
  615.1 3.9 collective-permute-start.26
  619.0 1.9 collective-permute-start.27
  621.1 1.0 collective-permute-done.27
  624.0 23.6 %all-reduce.20 = (f32[8]{0:T(128)S(1)}, f32[8]{0:T(128)S(1)}) all-reduce(f32[8]{0:T(128)S(1)} %reduce_sum.118, f32[8]{0:T(128)S(1)} %reduce_sum.119), channel_id=1, replica_groups=mesh['gx'=16,'gy'=32] {'gx'}, use_global_device_ids=true, to_apply=%region_25.26 | all-reduce | flops 16 | bytes 128 | tf_op jit(solution)/shard_map/psum | solution.py:126
  647.6 69.4 %all-reduce.17 = (f32[8]{0:T(128)S(1)}, f32[8]{0:T(128)S(1)}) all-reduce(f32[8]{0:T(128)S(1)} %get-tuple-element.20, f32[8]{0:T(128)S(1)} %get-tuple-element.21), channel_id=1, replica_groups=mesh['gx'=16,'gy'=32] {'gy'}, use_global_device_ids=true, to_apply=%region_26.27 | all-reduce | flops 16 | bytes 128 | tf_op jit(solution)/shard_map/psum | solution.py:125
  (170 shorter events, 25.4 us)
Async XLA Ops:
  0.6 8.3 %copy-start.1 = (f32[4,16,256]{2,1,0:T(8,128)S(1)}, f32[4,16,256]{2,1,0:T(8,128)}, u32[]{:S(2)}) copy-start(f32[4,16,256]{2,1,0:T(8,128)} %param.6) | copy-start | bytes 196612
  2.0 14.5 %collective-permute-start = (f32[1,16,256]{2,1,0:T(8,128)}, f32[1,16,256]{2,1,0:T(8,128)S(1)}, u32[]{:S(2)}, u32[]{:S(2)}) collective-permute-start(f32[1,16,256]{2,1,0:T(8,128)} %get-tuple-element.84), channel_id=1, source_target_pairs={{32,0},{64,32},{96,64},{128,96},{160,128},{192,160},{224,192},{256... | collective-permute-start | bytes 49160 | tf_op jit(solution)/shard_map/ppermute | solution.py:25
  3.3 12.4 %collective-permute-start.1 = (f32[1,16,256]{2,1,0:T(8,128)}, f32[1,16,256]{2,1,0:T(8,128)}, u32[]{:S(2)}, u32[]{:S(2)}) collective-permute-start(f32[1,16,256]{2,1,0:T(8,128)} %get-tuple-element.85), channel_id=1, source_target_pairs={{0,32},{32,64},{64,96},{96,128},{128,160},{160,192},{192,224},{224... | collective-permute-start | bytes 49160 | tf_op jit(solution)/shard_map/ppermute | solution.py:24
  8.9 2.4 copy-start.7
  9.6 1.1 copy-start.14
  9.6 1.7 copy-start.6
  9.6 1.7 copy-start.5
  11.3 0.7 copy-start.4
  14.3 0.6 copy-start.10
  14.3 0.7 copy-start.11
  15.0 0.7 copy-start.12
  15.0 0.7 copy-start.13
  17.1 13.4 %collective-permute-start.2 = (f32[6,1,256]{2,1,0:T(1,128)}, f32[6,1,256]{2,1,0:T(1,128)}, u32[]{:S(2)}, u32[]{:S(2)}) collective-permute-start(f32[6,1,256]{2,1,0:T(1,128)} %get-tuple-element.56), channel_id=1, source_target_pairs={{1,0},{2,1},{3,2},{4,3},{5,4},{6,5},{7,6},{8,7},{9,8},{10,9},{11,1... | collective-permute-start | bytes 18440 | tf_op jit(solution)/shard_map/ppermute | solution.py:25
  25.4 5.1 collective-permute-start.3
  29.3 1.1 copy-start
  30.3 0.8 copy-start.2
  30.3 0.9 copy-start.3
  30.3 0.9 copy-start.9
  30.5 0.7 copy-start.8
  32.1 2.6 collective-permute-start.5
  33.4 4.5 collective-permute-start.4
  37.8 7.1 collective-permute-start.6
  42.0 3.1 collective-permute-start.7
  158.1 2.6 collective-permute-start.9
  159.4 4.5 collective-permute-start.8
  163.9 6.2 collective-permute-start.10
  168.1 3.1 collective-permute-start.11
  266.1 2.6 collective-permute-start.13
  267.4 4.5 collective-permute-start.12
  271.9 6.6 collective-permute-start.14
  275.6 3.1 collective-permute-start.15
  383.7 2.6 collective-permute-start.17
  385.0 4.5 collective-permute-start.16
  389.5 5.9 collective-permute-start.18
  393.4 3.1 collective-permute-start.19
  491.5 2.6 collective-permute-start.21
  492.8 4.5 collective-permute-start.20
  497.3 6.6 collective-permute-start.22
  501.0 3.1 collective-permute-start.23
  609.3 2.6 collective-permute-start.25
  610.6 4.5 collective-permute-start.24
  615.1 5.9 collective-permute-start.26
  619.0 3.1 collective-permute-start.27
